TPU v7x, 256 devices: a whole 4x4x8 slice. The times are simulated.
256 devices in a mesh: seg: 8 (over y, core), ep: 32 (over z, x).
Axes of the slice: x: 4, y: 4, z: 8, core: 2. Of those that a mesh axis runs over, the one named last changes fastest.
Arguments:
- queries: bfloat16 [16384, 8192], P(('seg', 'ep')), may hold values from -6 to 6
- keys: bfloat16 [16384, 8192], P(('seg', 'ep')), may hold values from -1.25 to 1.25
- values: bfloat16 [16384, 8192], P(('seg', 'ep')), may hold values from -54 to 54
- log_decay: float32 [16384, 64], P('seg', 'ep'), may hold values from -1 to 0
- out_gain: float32 [8192], replicated, may hold values from 0.1 to 1.9
- out_proj: bfloat16 [8192, 6144], P('ep', 'seg'), may hold values from -0.0625 to 0.0625
- experts: int32 [2048, 2], P(('seg', 'ep')), may hold values from 0 to 15, all different within a row; in each aligned block of 8 rows (0 to 7, 8 to 15, ...) at most 2 rows name the same one
- gates: float32 [2048, 2], P(('seg', 'ep')), may hold values from 0.2 to 1
- up_weight: bfloat16 [32, 6144, 2304], P('ep', None, 'seg'), may hold values from -0.078125 to 0.078125
- down_weight: bfloat16 [32, 2304, 6144], P('ep', 'seg'), may hold values from -0.09375 to 0.09375
Outputs:
- attn_out: bfloat16 [16384, 8192], P(('seg', 'ep'))
- moe_out: bfloat16 [2048, 6144], P(('seg', 'ep'))
Inputs may be any that keep to these rules, and one draw needn't show every extreme that they name: Each row names two different experts. The 8 rows of one device name any one expert at most 2 times, and in some devices one expert exactly 2 times.
All inputs are finite; a program needn't handle non-finite values.
Results may differ from a plain program's by a relative error of at most 0.025.
Values may be sent and summed in bfloat16 or wider, within the bound.
No kernel may reach another device: no remote copies, remote signals or barrier semaphores. Data moves between devices by JAX's collectives and lax.ppermute only.
A program may use at most 128 MiB of HBM per device.

v0:
```python
import math
import jax
import jax.numpy as jnp
from jax import lax
from jax.sharding import Mesh
from jax.sharding import PartitionSpec as P

EP = ("ep_0", "ep_1")
SEG_EP = ("seg", "ep_0", "ep_1")
epsilon = 1e-06


def side_by_side(arrays, axis, dim, along):
    columns = [a.reshape(*a.shape[:along], -1) for a in arrays]
    both = jnp.concatenate(columns, axis=along)
    whole, at, done = (lax.all_gather(both, axis, axis=dim, tiled=True), 0, [])
    for a, column in zip(arrays, columns):
        section = whole[..., at : at + column.shape[along]]
        done.append(section.reshape(*section.shape[:along], *a.shape[along:]))
        at += column.shape[along]
    return tuple(done)


def sent_to_all(x, axis):
    devices = lax.axis_size(axis)
    return lax.all_to_all(jnp.broadcast_to(x[None], (devices, *x.shape)), axis, 0, 0, tiled=True)


def taken_together(x, axis):
    return sent_to_all(x, axis).sum(axis=0)


def scatter_axes(x, axes, dim):
    for axis in axes:
        x = lax.psum_scatter(x, axis, scatter_dimension=dim, tiled=True)
    return x


def route_tables(experts, gates, expert_count, capacity):
    token_count = experts.shape[0]
    flattened = experts.reshape(-1)
    onehot = (flattened[:, None] == jnp.arange(expert_count, dtype=jnp.int32)[None, :]).astype(
        jnp.int32
    )
    earlier = jnp.cumsum(onehot, axis=0) - onehot
    position = jnp.sum(earlier * onehot, axis=1)
    slot_index = (flattened * capacity + position).reshape(token_count, 2)
    columns = jnp.arange(expert_count * capacity, dtype=jnp.int32)
    matches = slot_index[:, :, None] == columns[None, None, :]
    dispatch = jnp.any(matches, axis=1).T.astype(jnp.bfloat16)
    combine = jnp.sum(jnp.where(matches, gates[:, :, None], 0.0), axis=1)
    return (dispatch, combine)


def expert_output(row_data, up_piece, down_piece):
    hidden = jax.nn.silu(jnp.dot(row_data, up_piece, preferred_element_type=jnp.float32)).astype(
        jnp.bfloat16
    )
    return jnp.dot(hidden, down_piece, preferred_element_type=jnp.float32)


def on_device(
    queries, keys, values, log_decay, out_gain, out_proj, experts, gates, up_weight, down_weight
):
    ep_count = lax.axis_size(EP)
    heads_local = log_decay.shape[1]
    head_dim = queries.shape[1] // (heads_local * ep_count)
    query_heads, key_heads, value_heads = (
        lax.all_to_all(queries, EP, split_axis=1, concat_axis=0, tiled=True),
        lax.all_to_all(keys, EP, split_axis=1, concat_axis=0, tiled=True),
        lax.all_to_all(values, EP, split_axis=1, concat_axis=0, tiled=True),
    )
    seg_length = query_heads.shape[0]
    query_heads = query_heads.reshape(seg_length, heads_local, head_dim)
    key_heads = key_heads.reshape(seg_length, heads_local, head_dim)
    value_heads = value_heads.reshape(seg_length, heads_local, head_dim)
    cumulative = jnp.cumsum(log_decay, axis=0)
    across = cumulative.T
    block_size = math.gcd(seg_length, 512)
    starts = jnp.arange(seg_length // block_size, dtype=jnp.int32) * block_size
    token_positions = jnp.arange(seg_length, dtype=jnp.int32)

    def block_mix(start):
        query_block = lax.dynamic_slice_in_dim(query_heads, start, block_size, 0)
        cum_block = lax.dynamic_slice_in_dim(across, start, block_size, 1)
        row_ids = start + jnp.arange(block_size, dtype=jnp.int32)
        causal = (row_ids[:, None] >= token_positions[None, :])[None]
        log_gap = cum_block[:, :, None] - across[:, None, :]
        weight = jnp.where(causal, jnp.exp(jnp.where(causal, log_gap, 0.0)), 0.0)
        scores = jnp.einsum(
            "thd,shd->hts", query_block, key_heads, preferred_element_type=jnp.float32
        )
        mixing = (scores * weight).astype(jnp.bfloat16)
        return jnp.einsum("hts,she->the", mixing, value_heads, preferred_element_type=jnp.float32)

    inside = lax.map(block_mix, starts).reshape(seg_length, heads_local, head_dim)
    ending = cumulative[-1]
    to_end = jnp.exp(ending[None, :] - cumulative)
    key_float = key_heads.astype(jnp.float32)
    value_float = value_heads.astype(jnp.float32)
    local_state = jnp.einsum("sh,shd,she->hde", to_end, key_float, value_float)
    all_ends, all_states = tuple(
        (
            part.astype(jnp.float32)
            for part in side_by_side(
                (ending[None].astype(jnp.bfloat16), local_state[None].astype(jnp.bfloat16)),
                "seg",
                0,
                2,
            )
        )
    )
    own_group = lax.axis_index("seg")
    group_ids = jnp.arange(all_ends.shape[0], dtype=jnp.int32)
    before = (group_ids < own_group)[:, None]
    through = jnp.cumsum(all_ends, axis=0)
    reaching = jnp.sum(jnp.where(before, all_ends, 0.0), axis=0)
    factors = jnp.where(before, jnp.exp(jnp.where(before, reaching[None, :] - through, 0.0)), 0.0)
    carried = jnp.einsum("gh,ghde->hde", factors, all_states)
    outside = jnp.exp(cumulative)[:, :, None] * jnp.einsum(
        "thd,hde->the", query_heads.astype(jnp.float32), carried
    )
    mixture = (inside + outside).astype(jnp.bfloat16).reshape(seg_length, heads_local * head_dim)
    token_mix = lax.all_to_all(mixture, EP, split_axis=0, concat_axis=1, tiled=True)
    as_float = token_mix.astype(jnp.float32)
    inv_rms = lax.rsqrt(jnp.mean(as_float * as_float, axis=1, keepdims=True) + epsilon)
    attn_out = (as_float * inv_rms * out_gain[None, :]).astype(jnp.bfloat16)
    row_stride = 8
    own_width = heads_local * head_dim
    feature_count = own_width * ep_count
    picked_float = mixture.reshape(seg_length // row_stride, row_stride, own_width)[:, 0].astype(
        jnp.float32
    )
    square_sums = taken_together(jnp.sum(picked_float * picked_float, axis=1), EP)
    picked_rms = lax.rsqrt(square_sums[:, None] / feature_count + epsilon)
    gain_slice = lax.dynamic_slice_in_dim(out_gain, lax.axis_index(EP) * own_width, own_width, 0)
    normed_rows = (picked_float * picked_rms * gain_slice[None, :]).astype(jnp.bfloat16)
    proj_terms = jnp.dot(
        normed_rows,
        lax.all_gather(out_proj, "seg", axis=1, tiled=True),
        preferred_element_type=jnp.float32,
    )
    moe_in = (
        scatter_axes(proj_terms.astype(jnp.bfloat16), EP, 0)
        .astype(jnp.float32)
        .astype(jnp.bfloat16)
    )
    expert_count = ep_count // 2
    token_count, model_width = moe_in.shape
    capacity = max(2, 4 * token_count // expert_count)
    dispatch, combine = route_tables(experts, gates, expert_count, capacity)
    up_piece = up_weight[0]
    down_piece = down_weight[0]
    slot_rows = jnp.dot(dispatch, moe_in, preferred_element_type=jnp.float32).astype(jnp.bfloat16)
    outgoing = jnp.repeat(slot_rows.reshape(expert_count, capacity, model_width), 2, axis=0)
    arrived = lax.all_to_all(outgoing, EP, split_axis=0, concat_axis=0, tiled=True).reshape(
        ep_count * capacity, model_width
    )
    gathered = lax.all_gather(arrived, "seg", axis=0, tiled=True)
    owned_sums = lax.psum_scatter(
        expert_output(gathered, up_piece, down_piece).astype(jnp.bfloat16),
        "seg",
        scatter_dimension=0,
        tiled=True,
    ).astype(jnp.float32)
    returned_back = lax.all_to_all(
        owned_sums.reshape(ep_count, capacity, model_width).astype(jnp.bfloat16),
        EP,
        split_axis=0,
        concat_axis=0,
        tiled=True,
    ).astype(jnp.float32)
    paired = returned_back.reshape(expert_count, 2, capacity, model_width)
    halves = (paired[:, 0] + paired[:, 1]).reshape(expert_count * capacity, model_width)
    summed = jnp.dot(combine, halves)
    moe_out = summed.astype(jnp.bfloat16)
    return (attn_out, moe_out)


def solution(mesh):
    torus = Mesh(mesh.devices.reshape(mesh.shape["seg"], 8, 4), ("seg", "ep_0", "ep_1"))
    placed = (
        P(SEG_EP, None),
        P(SEG_EP, None),
        P(SEG_EP, None),
        P("seg", EP),
        P(),
        P(EP, "seg"),
        P(SEG_EP, None),
        P(SEG_EP, None),
        P(EP, None, "seg"),
        P(EP, "seg", None),
    )
    return jax.shard_map(
        on_device,
        mesh=torus,
        in_specs=placed,
        out_specs=(P(SEG_EP, None), P(SEG_EP, None)),
        check_vma=False,
    )
```

profile of v0, /device:TPU:2, one launch (start us, length us, event | category | flops | bytes accessed | tf_op | source)
XLA Modules:
  0.0 520.2 jit_solution(4376102759249833830)
XLA Ops:
  7.2 2.5 copy.199
  9.7 11.8 %all-to-all-start.1 = ((bf16[64,32,256]{2,0,1:T(8,128)(2,1)}), bf16[64,32,256]{2,0,1:T(8,128)(2,1)}, u32[]{:S(2)}, u32[]{:S(2)}) async-start(bf16[64,32,256]{2,0,1:T(8,128)(2,1)} %bitcast.112), calls=%async_computation.1 | async-start | bytes 2097152 | tf_op jit(solution)/shard_map/all_to_all | solution.py:70
  21.5 2.3 copy.198
  23.8 25.8 %all-to-all-done.1 = bf16[64,32,256]{2,0,1:T(8,128)(2,1)} async-done(((bf16[64,32,256]{2,0,1:T(8,128)(2,1)}), bf16[64,32,256]{2,0,1:T(8,128)(2,1)}, u32[]{:S(2)}, u32[]{:S(2)}) %all-to-all-start.1) | async-done | bytes 1048608 | tf_op jit(solution)/shard_map/all_to_all | solution.py:70
  49.6 5.6 %all-to-all-start.2 = ((bf16[64,32,256]{2,0,1:T(8,128)(2,1)}), bf16[64,32,256]{2,0,1:T(8,128)(2,1)}, u32[]{:S(2)}, u32[]{:S(2)}) async-start(bf16[64,32,256]{2,0,1:T(8,128)(2,1)} %bitcast.110), calls=%async_computation.2 | async-start | bytes 2097152 | tf_op jit(solution)/shard_map/all_to_all | solution.py:71
  64.1 2.3 copy.200
  67.8 2.2 reshape.156
  70.0 12.2 %all-to-all-done.2 = bf16[64,32,256]{2,0,1:T(8,128)(2,1)} async-done(((bf16[64,32,256]{2,0,1:T(8,128)(2,1)}), bf16[64,32,256]{2,0,1:T(8,128)(2,1)}, u32[]{:S(2)}, u32[]{:S(2)}) %all-to-all-start.2) | async-done | bytes 1048608 | tf_op jit(solution)/shard_map/all_to_all | solution.py:71
  82.3 5.6 %all-to-all-start = ((bf16[64,32,256]{2,0,1:T(8,128)(2,1)}), bf16[64,32,256]{2,0,1:T(8,128)(2,1)}, u32[]{:S(2)}, u32[]{:S(2)}) async-start(bf16[64,32,256]{2,0,1:T(8,128)(2,1)} %bitcast.111), calls=%async_computation | async-start | bytes 2097152 | tf_op jit(solution)/shard_map/all_to_all | solution.py:69
  87.9 2.2 reshape.159
  90.1 5.6 %convert_multiply_fusion.1 = bf16[2048,2,128]{2,1,0:T(2,128)(2,1)S(1)} fusion(bf16[2048,2,128]{2,1,0:T(2,128)(2,1)} %reshape.156, f32[2048,2]{1,0:T(8,128)} %copy.139), kind=kLoop, calls=%fused_computation.27 | loop fusion | flops 1572864 | bytes 2113536 | tf_op jit(solution)/shard_map/sh,shd,she->hde/dot_general | solution.py:101
  95.7 2.5 fusion.18
  98.2 1.5 reshape.162
  100.7 13.8 %all_gather.9 = bf16[8,2,16385]{2,1,0:T(2,128)(2,1)S(1)} all-gather(bf16[1,2,16385]{2,1,0:T(2,128)(2,1)S(1)} %pad_maximum_fusion), channel_id=1, replica_groups=mesh['seg'=8,'ep_0'=8,'ep_1'=4] {'seg'}, dimensions={0}, use_global_device_ids=true | all-gather | bytes 589860 | tf_op jit(solution)/shard_map/all_gather | solution.py:16
  116.0 2.4 copy.136
  120.3 2.2 reshape.163
  122.6 2.1 reshape.155
  124.7 2.3 copy.135
  127.0 99.5 %while.11 = (s32[]{:T(128)}, f32[4,512,2,128]{1,0,3,2:T(4,128)}, s32[4]{0:T(128)S(1)}, bf16[2048,2,128]{2,0,1:T(8,128)(2,1)}, bf16[2048,2,128]{2,0,1:T(8,128)(2,...) while((s32[]{:T(128)}, f32[4,512,2,128]{1,0,3,2:T(4,128)}, ...), condition=%wide.region_3.4_spmd.clone, body=%wide.region_2.3_spmd.clone.sunk | while | flops 1085276672 | bytes 7110819 | solution.py:96
  130.6 1.7 iota_compare_fusion.5
  132.3 6.6 %fusion.58 = f32[1,512,2,128]{3,1,2,0:T(8,128)} fusion(bf16[2048,2,128]{2,0,1:T(8,128)(2,1)} %get-tuple-element.204, bf16[2048,2,128]{2,0,1:T(8,128)(2,1)} %get-tuple-element.202, f32[2,2048]{1,0:T(2,128)} %get-tuple-element.203, f32[2,512]{1,0:T(2,128)S(1)} %constant_dynamic-slice_fusion.2, pred[512,2048]{1,0:T(8,128)(4,1)} %iota_compare_fusion.5, ...), kind=kOutput, calls=%fused_computation.4.clone.1 | convolution fusion | flops 1084227584 | bytes 3952644 | tf_op jit(solution)/shard_map/while/body/eval_jaxpr/hts,she->the/dot_general | solution.py:94
  138.9 1.9 copy.204
  140.8 11.1 %dynamic_update_slice.6 = f32[4,512,2,128]{1,0,3,2:T(4,128)} dynamic-update-slice(f32[4,512,2,128]{1,0,3,2:T(4,128)} %get-tuple-element.189, f32[1,512,2,128]{1,0,3,2:T(1,128)} %copy.204, s32[]{:T(128)} %get-tuple-element.188, s32[]{:T(128)} %constant.22.clone.1..sunk, s32[]{:T(128)} %constant.22.clone.1..sunk, s32[]{:T(128)} %constant.22.clone.1..sunk) | dynamic-update-slice | bytes 1048580 | tf_op jit(solution)/shard_map/while/body/jit(dynamic_update_index_in_dim)/dynamic_update_slice | solution.py:96
  155.4 1.7 iota_compare_fusion.5
  157.2 6.6 %fusion.58 = f32[1,512,2,128]{3,1,2,0:T(8,128)} fusion(bf16[2048,2,128]{2,0,1:T(8,128)(2,1)} %get-tuple-element.204, bf16[2048,2,128]{2,0,1:T(8,128)(2,1)} %get-tuple-element.202, f32[2,2048]{1,0:T(2,128)} %get-tuple-element.203, f32[2,512]{1,0:T(2,128)S(1)} %constant_dynamic-slice_fusion.2, pred[512,2048]{1,0:T(8,128)(4,1)} %iota_compare_fusion.5, ...), kind=kOutput, calls=%fused_computation.4.clone.1 | convolution fusion | flops 1084227584 | bytes 3952644 | tf_op jit(solution)/shard_map/while/body/eval_jaxpr/hts,she->the/dot_general | solution.py:94
  163.7 1.9 copy.204
  165.7 11.1 %dynamic_update_slice.6 = f32[4,512,2,128]{1,0,3,2:T(4,128)} dynamic-update-slice(f32[4,512,2,128]{1,0,3,2:T(4,128)} %get-tuple-element.189, f32[1,512,2,128]{1,0,3,2:T(1,128)} %copy.204, s32[]{:T(128)} %get-tuple-element.188, s32[]{:T(128)} %constant.22.clone.1..sunk, s32[]{:T(128)} %constant.22.clone.1..sunk, s32[]{:T(128)} %constant.22.clone.1..sunk) | dynamic-update-slice | bytes 1048580 | tf_op jit(solution)/shard_map/while/body/jit(dynamic_update_index_in_dim)/dynamic_update_slice | solution.py:96
  180.3 1.7 iota_compare_fusion.5
  182.0 6.6 %fusion.58 = f32[1,512,2,128]{3,1,2,0:T(8,128)} fusion(bf16[2048,2,128]{2,0,1:T(8,128)(2,1)} %get-tuple-element.204, bf16[2048,2,128]{2,0,1:T(8,128)(2,1)} %get-tuple-element.202, f32[2,2048]{1,0:T(2,128)} %get-tuple-element.203, f32[2,512]{1,0:T(2,128)S(1)} %constant_dynamic-slice_fusion.2, pred[512,2048]{1,0:T(8,128)(4,1)} %iota_compare_fusion.5, ...), kind=kOutput, calls=%fused_computation.4.clone.1 | convolution fusion | flops 1084227584 | bytes 3952644 | tf_op jit(solution)/shard_map/while/body/eval_jaxpr/hts,she->the/dot_general | solution.py:94
  188.6 1.9 copy.204
  190.5 11.1 %dynamic_update_slice.6 = f32[4,512,2,128]{1,0,3,2:T(4,128)} dynamic-update-slice(f32[4,512,2,128]{1,0,3,2:T(4,128)} %get-tuple-element.189, f32[1,512,2,128]{1,0,3,2:T(1,128)} %copy.204, s32[]{:T(128)} %get-tuple-element.188, s32[]{:T(128)} %constant.22.clone.1..sunk, s32[]{:T(128)} %constant.22.clone.1..sunk, s32[]{:T(128)} %constant.22.clone.1..sunk) | dynamic-update-slice | bytes 1048580 | tf_op jit(solution)/shard_map/while/body/jit(dynamic_update_index_in_dim)/dynamic_update_slice | solution.py:96
  205.2 1.7 iota_compare_fusion.5
  206.9 6.6 %fusion.58 = f32[1,512,2,128]{3,1,2,0:T(8,128)} fusion(bf16[2048,2,128]{2,0,1:T(8,128)(2,1)} %get-tuple-element.204, bf16[2048,2,128]{2,0,1:T(8,128)(2,1)} %get-tuple-element.202, f32[2,2048]{1,0:T(2,128)} %get-tuple-element.203, f32[2,512]{1,0:T(2,128)S(1)} %constant_dynamic-slice_fusion.2, pred[512,2048]{1,0:T(8,128)(4,1)} %iota_compare_fusion.5, ...), kind=kOutput, calls=%fused_computation.4.clone.1 | convolution fusion | flops 1084227584 | bytes 3952644 | tf_op jit(solution)/shard_map/while/body/eval_jaxpr/hts,she->the/dot_general | solution.py:94
  213.5 1.9 copy.204
  215.4 11.1 %dynamic_update_slice.6 = f32[4,512,2,128]{1,0,3,2:T(4,128)} dynamic-update-slice(f32[4,512,2,128]{1,0,3,2:T(4,128)} %get-tuple-element.189, f32[1,512,2,128]{1,0,3,2:T(1,128)} %copy.204, s32[]{:T(128)} %get-tuple-element.188, s32[]{:T(128)} %constant.22.clone.1..sunk, s32[]{:T(128)} %constant.22.clone.1..sunk, s32[]{:T(128)} %constant.22.clone.1..sunk) | dynamic-update-slice | bytes 1048580 | tf_op jit(solution)/shard_map/while/body/jit(dynamic_update_index_in_dim)/dynamic_update_slice | solution.py:96
  226.5 3.7 reshape.160
  231.7 1.4 fusion.23
  233.2 3.4 fusion.14
  236.6 3.7 copy.145
  240.3 2.5 reshape_reshape.3
  245.6 9.8 %all-to-all-start.4 = ((f32[32,1,256]{2,1,0:T(1,128)}), f32[32,1,256]{2,1,0:T(1,128)}, u32[]{:S(2)}, u32[]{:S(2)}) async-start(f32[32,1,256]{2,1,0:T(1,128)} %broadcast_in_dim.85), calls=%async_computation.4 | async-start | bytes 65536 | tf_op jit(solution)/shard_map/all_to_all | solution.py:26
  256.3 7.8 %all-to-all-done.4 = f32[32,1,256]{2,1,0:T(1,128)} async-done(((f32[32,1,256]{2,1,0:T(1,128)}), f32[32,1,256]{2,1,0:T(1,128)}, u32[]{:S(2)}, u32[]{:S(2)}) %all-to-all-start.4) | async-done | bytes 32800 | tf_op jit(solution)/shard_map/all_to_all | solution.py:26
  265.0 4.7 convolution_convert_fusion.1
  269.8 41.9 %reduce-scatter.4.cloned.1.call-done = bf16[32,6144]{1,0:T(8,128)(2,1)} async-done(((bf16[256,6144]{1,0:T(8,128)(2,1)}), bf16[32,6144]{1,0:T(8,128)(2,1)}) %reduce-scatter.4.cloned.1.call-update) | async-done | bytes 393232 | tf_op jit(solution)/shard_map/reduce_scatter | solution.py:35
  315.2 19.9 %reduce-scatter.6.cloned.1.call-done = bf16[8,6144]{1,0:T(8,128)(2,1)} async-done(((bf16[32,6144]{1,0:T(8,128)(2,1)}), bf16[8,6144]{1,0:T(8,128)(2,1)}) %reduce-scatter.6.cloned.1.call-update) | async-done | bytes 98320 | tf_op jit(solution)/shard_map/reduce_scatter | solution.py:35
  335.0 1.9 convolution_convert_fusion.2
  337.0 2.0 reshape.164
  340.4 30.7 %all_to_all.77 = bf16[32,2,6144]{2,1,0:T(2,128)(2,1)} all-to-all(bf16[32,2,6144]{2,1,0:T(2,128)(2,1)S(1)} %bitcast.113), channel_id=1, replica_groups=mesh['seg'=8,'ep_0'=8,'ep_1'=4] {'ep_0','ep_1'}, dimensions={0} | all-to-all | bytes 1572864 | tf_op jit(solution)/shard_map/all_to_all | solution.py:156
  371.2 3.0 reshape.166
  374.2 40.3 %all-gather.5.cloned.1.call-done = bf16[512,6144]{1,0:T(8,128)(2,1)} async-done(((bf16[64,6144]{1,0:T(8,128)(2,1)}), bf16[512,6144]{1,0:T(8,128)(2,1)}) %all-gather.5.cloned.1.call-update) | async-done | bytes 6291472 | tf_op jit(solution)/shard_map/all_gather | solution.py:159
  414.5 12.0 %convolution_convert_fusion = bf16[512,6144]{1,0:T(8,128)(2,1)} fusion(bf16[1,288,6144]{2,1,0:T(8,128)(2,1)S(1)} %copy-done, bf16[512,6144]{1,0:T(8,128)(2,1)} %all-gather.5.cloned.1.call-done, bf16[1,6144,288]{1,2,0:T(8,128)(2,1)} %param.20), kind=kOutput, calls=%fused_computation.10 | convolution fusion | flops 3627761664 | bytes 19660800 | tf_op jit(solution)/shard_map/dot_general | solution.py:59
  426.6 2.5 all_to_all.65
  429.1 10.2 %all-to-all-start.3 = ((bf16[32,64,256]{2,1,0:T(8,128)(2,1)}), bf16[32,64,256]{2,1,0:T(8,128)(2,1)}, u32[]{:S(2)}, u32[]{:S(2)}) async-start(bf16[32,64,256]{2,1,0:T(8,128)(2,1)} %all_to_all.65), calls=%async_computation.3 | async-start | bytes 2097152 | tf_op jit(solution)/shard_map/all_to_all | solution.py:124
  439.4 28.5 %all-to-all-done.3 = bf16[32,64,256]{2,1,0:T(8,128)(2,1)} async-done(((bf16[32,64,256]{2,1,0:T(8,128)(2,1)}), bf16[32,64,256]{2,1,0:T(8,128)(2,1)}, u32[]{:S(2)}, u32[]{:S(2)}) %all-to-all-start.3) | async-done | bytes 1048608 | tf_op jit(solution)/shard_map/all_to_all | solution.py:124
  467.9 1.5 convert_bitcast_fusion
  469.3 1.5 copy.171
  470.9 1.6 fusion.15
  472.5 2.9 convert_element_type.93
  475.3 9.8 %all-to-all-start.6 = ((bf16[32,2,6144]{2,1,0:T(2,128)(2,1)}), bf16[32,2,6144]{2,1,0:T(2,128)(2,1)}, u32[]{:S(2)}, u32[]{:S(2)}) async-start(bf16[32,2,6144]{2,1,0:T(2,128)(2,1)} %convert_element_type.93), calls=%async_computation.9 | async-start | bytes 1572864 | tf_op jit(solution)/shard_map/all_to_all | solution.py:166
  485.2 2.8 multiply_convert_fusion.1
  488.0 18.8 %all-to-all-done.6 = bf16[32,2,6144]{2,1,0:T(2,128)(2,1)} async-done(((bf16[32,2,6144]{2,1,0:T(2,128)(2,1)}), bf16[32,2,6144]{2,1,0:T(2,128)(2,1)}, u32[]{:S(2)}, u32[]{:S(2)}) %all-to-all-start.6) | async-done | bytes 786464 | tf_op jit(solution)/shard_map/all_to_all | solution.py:166
  506.8 2.0 convert.7
  509.9 1.9 add.80
  511.8 1.8 fusion.40
  (82 shorter events, 34.5 us)
Async XLA Ops:
  7.2 407.3 %copy-start = (bf16[1,288,6144]{2,1,0:T(8,128)(2,1)S(1)}, bf16[1,288,6144]{2,1,0:T(8,128)(2,1)}, u32[]{:S(2)}) copy-start(bf16[1,288,6144]{2,1,0:T(8,128)(2,1)} %param.21) | copy-start | bytes 10616836
  9.7 46.3 %copy-start.4 = (f32[2048,2]{0,1:T(2,128)S(1)}, f32[2048,2]{0,1:T(2,128)}, u32[]{:S(2)}) copy-start(f32[2048,2]{0,1:T(2,128)} %param.15) | copy-start | bytes 49156
  9.7 39.9 %all-to-all-start.1 = ((bf16[64,32,256]{2,0,1:T(8,128)(2,1)}), bf16[64,32,256]{2,0,1:T(8,128)(2,1)}, u32[]{:S(2)}, u32[]{:S(2)}) async-start(bf16[64,32,256]{2,0,1:T(8,128)(2,1)} %bitcast.112), calls=%async_computation.1 | async-start | bytes 2097152 | tf_op jit(solution)/shard_map/all_to_all | solution.py:70
  49.6 32.7 %all-to-all-start.2 = ((bf16[64,32,256]{2,0,1:T(8,128)(2,1)}), bf16[64,32,256]{2,0,1:T(8,128)(2,1)}, u32[]{:S(2)}, u32[]{:S(2)}) async-start(bf16[64,32,256]{2,0,1:T(8,128)(2,1)} %bitcast.110), calls=%async_computation.2 | async-start | bytes 2097152 | tf_op jit(solution)/shard_map/all_to_all | solution.py:71
  55.2 209.8 %all-gather.3.cloned.1.call-start = ((), (), s32[]{:S(2)}) async-start(), calls=%async_computation.10 | async-start | bytes 3538944 | tf_op jit(solution)/shard_map/all_gather | solution.py:140
  82.3 40.3 %all-to-all-start = ((bf16[64,32,256]{2,0,1:T(8,128)(2,1)}), bf16[64,32,256]{2,0,1:T(8,128)(2,1)}, u32[]{:S(2)}, u32[]{:S(2)}) async-start(bf16[64,32,256]{2,0,1:T(8,128)(2,1)} %bitcast.111), calls=%async_computation | async-start | bytes 2097152 | tf_op jit(solution)/shard_map/all_to_all | solution.py:69
  99.6 18.7 %copy-start.1 = (bf16[2048,2,128]{2,1,0:T(2,128)(2,1)S(1)}, bf16[2048,2,128]{2,1,0:T(2,128)(2,1)}, u32[]{:S(2)}) copy-start(bf16[2048,2,128]{2,1,0:T(2,128)(2,1)} %reshape.159) | copy-start | bytes 3145732
  119.6 7.4 %copy-start.7 = (bf16[8,2,1]{0,1,2:T(2,128)(2,1)}, bf16[8,2,1]{0,1,2:T(2,128)(2,1)S(1)}, u32[]{:S(2)}) copy-start(bf16[8,2,1]{0,1,2:T(2,128)(2,1)S(1)} %copy.159) | copy-start | bytes 100
  226.5 6.7 %copy-start.3 = (f32[2048,2]{0,1:T(2,128)S(1)}, f32[2048,2]{0,1:T(2,128)}, u32[]{:S(2)}) copy-start(f32[2048,2]{0,1:T(2,128)} %get-tuple-element.131) | copy-start | bytes 49156
  244.2 0.7 copy-start.2
  245.6 18.5 %all-to-all-start.4 = ((f32[32,1,256]{2,1,0:T(1,128)}), f32[32,1,256]{2,1,0:T(1,128)}, u32[]{:S(2)}, u32[]{:S(2)}) async-start(f32[32,1,256]{2,1,0:T(1,128)} %broadcast_in_dim.85), calls=%async_computation.4 | async-start | bytes 65536 | tf_op jit(solution)/shard_map/all_to_all | solution.py:26
  255.5 56.2 %reduce-scatter.4.cloned.1.call-start = ((), (), s32[]{:S(2)}) async-start(), calls=%async_computation.11 | async-start | bytes 3538944 | tf_op jit(solution)/shard_map/reduce_scatter | solution.py:35
  269.7 42.3 %copy-start.5 = (s32[8,2]{0,1:T(2,128)S(1)}, s32[8,2]{0,1:T(2,128)}, u32[]{:S(2)}) copy-start(s32[8,2]{0,1:T(2,128)} %param.18) | copy-start | bytes 196
  269.7 65.3 %reduce-scatter.6.cloned.1.call-start = ((), (), s32[]{:S(2)}) async-start(), calls=%async_computation.12 | async-start | bytes 491520 | tf_op jit(solution)/shard_map/reduce_scatter | solution.py:35
  311.7 102.8 %all-gather.5.cloned.1.call-start = ((), (), s32[]{:S(2)}) async-start(), calls=%async_computation.13 | async-start | bytes 7077888 | tf_op jit(solution)/shard_map/all_gather | solution.py:159
  374.1 98.3 %reduce-scatter.8.cloned.1.call-start = ((), (), s32[]{:S(2)}) async-start(), calls=%async_computation.14 | async-start | bytes 7077888 | tf_op jit(solution)/shard_map/reduce_scatter | solution.py:160
  426.6 12.8 %copy-start.6 = (f32[8,2]{0,1:T(2,128)S(1)}, f32[8,2]{0,1:T(2,128)}, u32[]{:S(2)}) copy-start(f32[8,2]{0,1:T(2,128)} %param.19) | copy-start | bytes 196
  429.1 38.7 %all-to-all-start.3 = ((bf16[32,64,256]{2,1,0:T(8,128)(2,1)}), bf16[32,64,256]{2,1,0:T(8,128)(2,1)}, u32[]{:S(2)}, u32[]{:S(2)}) async-start(bf16[32,64,256]{2,1,0:T(8,128)(2,1)} %all_to_all.65), calls=%async_computation.3 | async-start | bytes 2097152 | tf_op jit(solution)/shard_map/all_to_all | solution.py:124
  475.3 31.5 %all-to-all-start.6 = ((bf16[32,2,6144]{2,1,0:T(2,128)(2,1)}), bf16[32,2,6144]{2,1,0:T(2,128)(2,1)}, u32[]{:S(2)}, u32[]{:S(2)}) async-start(bf16[32,2,6144]{2,1,0:T(2,128)(2,1)} %convert_element_type.93), calls=%async_computation.9 | async-start | bytes 1572864 | tf_op jit(solution)/shard_map/all_to_all | solution.py:166
Sparse Core Ops, SparseCore 0:
  57.9 31.4 all-gather.2
  269.8 41.8 reduce-scatter.3
  314.2 20.7 reduce-scatter.5
  374.2 40.2 all-gather.4
  426.7 45.5 reduce-scatter.7
where the time goes:
time: 524 us; the launch traced here: 520 us
  waiting for transfers between devices  196 us (37%)
  local copies, waits for them, and re-layouts  115 us (22%)
  matrix products  54.1 us (10%)
  starting transfers between devices  53.3 us (10%)
  blocking collectives  44.5 us (8%)
  other arithmetic  36.2 us (7%)
  between operations  14 us (3%)
  loops' own time  6.62 us (1%)
    reduce_scatter x2, waiting for transfers between devices, scatter_axes(): x = lax.psum_scatter(x, axis, scatter_dimension=dim, tiled=True)  61.8 us
    dynamic_update_slice x8, local copies, waits for them, and re-layouts, on_device(): lax.map(block_mix, starts).reshape(seg_length, heads_local, head_dim)  52.2 us
    all_gather x1, waiting for transfers between devices, on_device(): gathered = lax.all_gather(arrived, 'seg', axis=0, tiled=True)  40.3 us
    all_to_all x1, blocking collectives, on_device(): lax.all_to_all(outgoing, EP, split_axis=0, concat_axis=0, tiled=True)  30.7 us
    all_to_all x1, waiting for transfers between devices, on_device(): lax.all_to_all(mixture, EP, split_axis=0, concat_axis=1, tiled=True)  28.5 us
    dot_general x4, matrix products, block_mix(): jnp.einsum('hts,she->the', mixing, value_heads, preferred_element_type=jn...  26.3 us
    all_to_all x1, waiting for transfers between devices, on_device(): lax.all_to_all(keys, EP, split_axis=1, concat_axis=0, tiled=True)  25.8 us
    all_to_all x1, waiting for transfers between devices, on_device(): lax.all_to_all(owned_sums.reshape(ep_count, capacity, model_width).astype...  18.8 us
  transfers between devices with their start and end apart: 11, of which 8 were waited for; matrix products, arithmetic and copies ran while one was open for 32% of the time, Pallas kernels for 0%

commit v1 on v0

--- a/solution.py
+++ b/solution.py
@@ -8,6 +8,12 @@
 EP = ("ep_0", "ep_1")
 SEG_EP = ("seg", "ep_0", "ep_1")
 epsilon = 1e-06
+
+
+def stacked_exchange(array, name, split, join):
+    cells = jnp.split(array, lax.axis_size(name), axis=split)
+    incoming = lax.all_to_all(jnp.stack(cells), name, 0, 0)
+    return jnp.concatenate(incoming, axis=join)
 
 
 def side_by_side(arrays, axis, dim, along):
@@ -67,7 +73,7 @@
     head_dim = queries.shape[1] // (heads_local * ep_count)
     query_heads, key_heads, value_heads = (
         lax.all_to_all(queries, EP, split_axis=1, concat_axis=0, tiled=True),
-        lax.all_to_all(keys, EP, split_axis=1, concat_axis=0, tiled=True),
+        stacked_exchange(keys, EP, 1, 0),
         lax.all_to_all(values, EP, split_axis=1, concat_axis=0, tiled=True),
     )
     seg_length = query_heads.shape[0]

time: 524 us -> 545 us (1.040)
  local copies, waits for them, and re-layouts: 115 us -> 156 us
  waiting for transfers between devices: 196 us -> 171 us
    unnamed x23 -> x56, local copies, waits for them, and re-layouts: 7.98 us -> 50.2 us
    all_to_all x1, waiting for transfers between devices: 25.8 us -> 12.8 us  [stacked_exchange(): incoming = lax.all_to_all(jnp.stack(cells), name, 0, 0)]
    all_to_all x1, waiting for transfers between devices: 12.2 us -> 0.01 us  [on_device(): lax.all_to_all(values, EP, split_axis=1, concat_axis=0, tiled=True)]
    all_to_all x1, starting transfers between devices: 5.62 us -> 11.8 us  [on_device(): lax.all_to_all(values, EP, split_axis=1, concat_axis=0, tiled=True)]
  transfers between devices with their start and end apart: 11 -> 11, of which waited for: 8 -> 7; matrix products, arithmetic and copies ran while one was open for 32% -> 38% of each run, Pallas kernels for 0% -> 0%
where the time goes in v1:
time: 545 us; the launch traced here: 539 us
  waiting for transfers between devices  171 us (31%)
  local copies, waits for them, and re-layouts  156 us (29%)
  starting transfers between devices  57.5 us (11%)
  matrix products  52.8 us (10%)
  blocking collectives  44.6 us (8%)
  other arithmetic  36.3 us (7%)
  between operations  14 us (3%)
  loops' own time  6.62 us (1%)
    reduce_scatter x2, waiting for transfers between devices, scatter_axes(): x = lax.psum_scatter(x, axis, scatter_dimension=dim, tiled=True)  61.8 us
    dynamic_update_slice x8, local copies, waits for them, and re-layouts, on_device(): lax.map(block_mix, starts).reshape(seg_length, heads_local, head_dim)  52.2 us
    unnamed x56, local copies, waits for them, and re-layouts  50.2 us
    all_gather x1, waiting for transfers between devices, on_device(): gathered = lax.all_gather(arrived, 'seg', axis=0, tiled=True)  40.3 us
    all_to_all x1, blocking collectives, on_device(): lax.all_to_all(outgoing, EP, split_axis=0, concat_axis=0, tiled=True)  30.7 us
    all_to_all x1, waiting for transfers between devices, on_device(): lax.all_to_all(mixture, EP, split_axis=0, concat_axis=1, tiled=True)  28.5 us
    dot_general x4, matrix products, block_mix(): jnp.einsum('hts,she->the', mixing, value_heads, preferred_element_type=jn...  26.3 us
    all_to_all x1, waiting for transfers between devices, on_device(): lax.all_to_all(owned_sums.reshape(ep_count, capacity, model_width).astype...  18.8 us
  transfers between devices with their start and end apart: 11, of which 7 were waited for; matrix products, arithmetic and copies ran while one was open for 38% of the time, Pallas kernels for 0%

profile of v1, /device:TPU:2, one launch (start us, length us, event | category | flops | bytes accessed | tf_op | source)
XLA Modules:
  0.0 539.1 jit_solution(18436154600168060661)
XLA Ops:
  7.2 2.5 copy.189
  9.7 11.8 %all-to-all-start.2 = ((bf16[64,32,256]{2,0,1:T(8,128)(2,1)}), bf16[64,32,256]{2,0,1:T(8,128)(2,1)}, u32[]{:S(2)}, u32[]{:S(2)}) async-start(bf16[64,32,256]{2,0,1:T(8,128)(2,1)} %bitcast.169), calls=%async_computation.2 | async-start | bytes 2097152 | tf_op jit(solution)/shard_map/all_to_all | solution.py:77
  65.0 9.8 %all-to-all-start.1 = ((bf16[32,64,256]{2,1,0:T(8,128)(2,1)}), bf16[32,64,256]{2,1,0:T(8,128)(2,1)}, u32[]{:S(2)}, u32[]{:S(2)}) async-start(bf16[32,64,256]{2,1,0:T(8,128)(2,1)} %constant_dynamic-update-slice_fusion), calls=%async_computation.1 | async-start | bytes 2097152 | tf_op jit(solution)/shard_map/all_to_all | solution.py:15
  78.2 1.4 reduce-window.9
  83.8 2.3 copy.190
  87.4 2.2 reshape.151
  89.6 12.8 %all-to-all-done.1 = bf16[32,64,256]{2,1,0:T(8,128)(2,1)} async-done(((bf16[32,64,256]{2,1,0:T(8,128)(2,1)}), bf16[32,64,256]{2,1,0:T(8,128)(2,1)}, u32[]{:S(2)}, u32[]{:S(2)}) %all-to-all-start.1) | async-done | bytes 1048608 | tf_op jit(solution)/shard_map/all_to_all | solution.py:15
  102.4 5.6 %all-to-all-start = ((bf16[64,32,256]{2,0,1:T(8,128)(2,1)}), bf16[64,32,256]{2,0,1:T(8,128)(2,1)}, u32[]{:S(2)}, u32[]{:S(2)}) async-start(bf16[64,32,256]{2,0,1:T(8,128)(2,1)} %bitcast.170), calls=%async_computation | async-start | bytes 2097152 | tf_op jit(solution)/shard_map/all_to_all | solution.py:75
  108.1 2.1 reshape_reshape.6
  110.2 5.7 %convert_multiply_fusion.1 = bf16[2048,2,128]{2,1,0:T(2,128)(2,1)S(1)} fusion(bf16[2048,2,128]{2,1,0:T(2,128)(2,1)} %reshape_reshape.6, f32[2048,2]{1,0:T(8,128)} %copy.132), kind=kLoop, calls=%fused_computation.27 | loop fusion | flops 1572864 | bytes 2113536 | tf_op jit(solution)/shard_map/sh,shd,she->hde/dot_general | solution.py:107
  117.1 1.5 reshape.154
  119.7 13.8 %all_gather.9 = bf16[8,2,16385]{2,1,0:T(2,128)(2,1)S(1)} all-gather(bf16[1,2,16385]{2,1,0:T(2,128)(2,1)S(1)} %pad_maximum_fusion), channel_id=1, replica_groups=mesh['seg'=8,'ep_0'=8,'ep_1'=4] {'seg'}, dimensions={0}, use_global_device_ids=true | all-gather | bytes 589860 | tf_op jit(solution)/shard_map/all_gather | solution.py:22
  133.5 1.4 slice.35
  134.9 2.4 copy.129
  139.3 2.2 reshape.155
  141.5 2.1 reshape.148
  143.7 2.3 copy.128
  146.0 99.4 %while.11 = (s32[]{:T(128)}, f32[4,512,2,128]{1,0,3,2:T(4,128)}, s32[4]{0:T(128)S(1)}, bf16[2048,2,128]{2,0,1:T(8,128)(2,1)}, bf16[2048,2,128]{2,0,1:T(8,128)(2,...) while((s32[]{:T(128)}, f32[4,512,2,128]{1,0,3,2:T(4,128)}, ...), condition=%wide.region_3.4_spmd.clone, body=%wide.region_2.3_spmd.clone.sunk | while | flops 1085276672 | bytes 7110819 | solution.py:102
  149.5 1.7 iota_compare_fusion.5
  151.3 6.6 %fusion.58 = f32[1,512,2,128]{3,1,2,0:T(8,128)} fusion(bf16[2048,2,128]{2,0,1:T(8,128)(2,1)} %get-tuple-element.204, bf16[2048,2,128]{2,0,1:T(8,128)(2,1)} %get-tuple-element.202, f32[2,2048]{1,0:T(2,128)} %get-tuple-element.203, f32[2,512]{1,0:T(2,128)S(1)} %constant_dynamic-slice_fusion.2, pred[512,2048]{1,0:T(8,128)(4,1)} %iota_compare_fusion.5, ...), kind=kOutput, calls=%fused_computation.4.clone.1 | convolution fusion | flops 1084227584 | bytes 3952644 | tf_op jit(solution)/shard_map/while/body/eval_jaxpr/hts,she->the/dot_general | solution.py:100
  157.8 1.9 copy.194
  159.8 11.1 %dynamic_update_slice.6 = f32[4,512,2,128]{1,0,3,2:T(4,128)} dynamic-update-slice(f32[4,512,2,128]{1,0,3,2:T(4,128)} %get-tuple-element.189, f32[1,512,2,128]{1,0,3,2:T(1,128)} %copy.194, s32[]{:T(128)} %get-tuple-element.188, s32[]{:T(128)} %constant.22.clone.1..sunk, s32[]{:T(128)} %constant.22.clone.1..sunk, s32[]{:T(128)} %constant.22.clone.1..sunk) | dynamic-update-slice | bytes 1048580 | tf_op jit(solution)/shard_map/while/body/jit(dynamic_update_index_in_dim)/dynamic_update_slice | solution.py:102
  174.4 1.7 iota_compare_fusion.5
  176.1 6.6 %fusion.58 = f32[1,512,2,128]{3,1,2,0:T(8,128)} fusion(bf16[2048,2,128]{2,0,1:T(8,128)(2,1)} %get-tuple-element.204, bf16[2048,2,128]{2,0,1:T(8,128)(2,1)} %get-tuple-element.202, f32[2,2048]{1,0:T(2,128)} %get-tuple-element.203, f32[2,512]{1,0:T(2,128)S(1)} %constant_dynamic-slice_fusion.2, pred[512,2048]{1,0:T(8,128)(4,1)} %iota_compare_fusion.5, ...), kind=kOutput, calls=%fused_computation.4.clone.1 | convolution fusion | flops 1084227584 | bytes 3952644 | tf_op jit(solution)/shard_map/while/body/eval_jaxpr/hts,she->the/dot_general | solution.py:100
  182.7 1.9 copy.194
  184.6 11.1 %dynamic_update_slice.6 = f32[4,512,2,128]{1,0,3,2:T(4,128)} dynamic-update-slice(f32[4,512,2,128]{1,0,3,2:T(4,128)} %get-tuple-element.189, f32[1,512,2,128]{1,0,3,2:T(1,128)} %copy.194, s32[]{:T(128)} %get-tuple-element.188, s32[]{:T(128)} %constant.22.clone.1..sunk, s32[]{:T(128)} %constant.22.clone.1..sunk, s32[]{:T(128)} %constant.22.clone.1..sunk) | dynamic-update-slice | bytes 1048580 | tf_op jit(solution)/shard_map/while/body/jit(dynamic_update_index_in_dim)/dynamic_update_slice | solution.py:102
  199.3 1.7 iota_compare_fusion.5
  201.0 6.6 %fusion.58 = f32[1,512,2,128]{3,1,2,0:T(8,128)} fusion(bf16[2048,2,128]{2,0,1:T(8,128)(2,1)} %get-tuple-element.204, bf16[2048,2,128]{2,0,1:T(8,128)(2,1)} %get-tuple-element.202, f32[2,2048]{1,0:T(2,128)} %get-tuple-element.203, f32[2,512]{1,0:T(2,128)S(1)} %constant_dynamic-slice_fusion.2, pred[512,2048]{1,0:T(8,128)(4,1)} %iota_compare_fusion.5, ...), kind=kOutput, calls=%fused_computation.4.clone.1 | convolution fusion | flops 1084227584 | bytes 3952644 | tf_op jit(solution)/shard_map/while/body/eval_jaxpr/hts,she->the/dot_general | solution.py:100
  207.6 1.9 copy.194
  209.5 11.1 %dynamic_update_slice.6 = f32[4,512,2,128]{1,0,3,2:T(4,128)} dynamic-update-slice(f32[4,512,2,128]{1,0,3,2:T(4,128)} %get-tuple-element.189, f32[1,512,2,128]{1,0,3,2:T(1,128)} %copy.194, s32[]{:T(128)} %get-tuple-element.188, s32[]{:T(128)} %constant.22.clone.1..sunk, s32[]{:T(128)} %constant.22.clone.1..sunk, s32[]{:T(128)} %constant.22.clone.1..sunk) | dynamic-update-slice | bytes 1048580 | tf_op jit(solution)/shard_map/while/body/jit(dynamic_update_index_in_dim)/dynamic_update_slice | solution.py:102
  224.1 1.7 iota_compare_fusion.5
  225.8 6.6 %fusion.58 = f32[1,512,2,128]{3,1,2,0:T(8,128)} fusion(bf16[2048,2,128]{2,0,1:T(8,128)(2,1)} %get-tuple-element.204, bf16[2048,2,128]{2,0,1:T(8,128)(2,1)} %get-tuple-element.202, f32[2,2048]{1,0:T(2,128)} %get-tuple-element.203, f32[2,512]{1,0:T(2,128)S(1)} %constant_dynamic-slice_fusion.2, pred[512,2048]{1,0:T(8,128)(4,1)} %iota_compare_fusion.5, ...), kind=kOutput, calls=%fused_computation.4.clone.1 | convolution fusion | flops 1084227584 | bytes 3952644 | tf_op jit(solution)/shard_map/while/body/eval_jaxpr/hts,she->the/dot_general | solution.py:100
  232.4 1.9 copy.194
  234.3 11.1 %dynamic_update_slice.6 = f32[4,512,2,128]{1,0,3,2:T(4,128)} dynamic-update-slice(f32[4,512,2,128]{1,0,3,2:T(4,128)} %get-tuple-element.189, f32[1,512,2,128]{1,0,3,2:T(1,128)} %copy.194, s32[]{:T(128)} %get-tuple-element.188, s32[]{:T(128)} %constant.22.clone.1..sunk, s32[]{:T(128)} %constant.22.clone.1..sunk, s32[]{:T(128)} %constant.22.clone.1..sunk) | dynamic-update-slice | bytes 1048580 | tf_op jit(solution)/shard_map/while/body/jit(dynamic_update_index_in_dim)/dynamic_update_slice | solution.py:102
  245.5 3.7 reshape.152
  250.7 1.4 fusion.23
  252.1 3.4 fusion.14
  255.5 3.7 copy.138
  259.2 2.5 reshape_reshape.7
  264.6 9.8 %all-to-all-start.4 = ((f32[32,1,256]{2,1,0:T(1,128)}), f32[32,1,256]{2,1,0:T(1,128)}, u32[]{:S(2)}, u32[]{:S(2)}) async-start(f32[32,1,256]{2,1,0:T(1,128)} %broadcast_in_dim.85), calls=%async_computation.4 | async-start | bytes 65536 | tf_op jit(solution)/shard_map/all_to_all | solution.py:32
  275.2 7.8 %all-to-all-done.4 = f32[32,1,256]{2,1,0:T(1,128)} async-done(((f32[32,1,256]{2,1,0:T(1,128)}), f32[32,1,256]{2,1,0:T(1,128)}, u32[]{:S(2)}, u32[]{:S(2)}) %all-to-all-start.4) | async-done | bytes 32800 | tf_op jit(solution)/shard_map/all_to_all | solution.py:32
  283.9 4.7 convolution_convert_fusion.1
  288.7 41.9 %reduce-scatter.4.cloned.1.call-done = bf16[32,6144]{1,0:T(8,128)(2,1)} async-done(((bf16[256,6144]{1,0:T(8,128)(2,1)}), bf16[32,6144]{1,0:T(8,128)(2,1)}) %reduce-scatter.4.cloned.1.call-update) | async-done | bytes 393232 | tf_op jit(solution)/shard_map/reduce_scatter | solution.py:41
  334.1 19.9 %reduce-scatter.6.cloned.1.call-done = bf16[8,6144]{1,0:T(8,128)(2,1)} async-done(((bf16[32,6144]{1,0:T(8,128)(2,1)}), bf16[8,6144]{1,0:T(8,128)(2,1)}) %reduce-scatter.6.cloned.1.call-update) | async-done | bytes 98320 | tf_op jit(solution)/shard_map/reduce_scatter | solution.py:41
  354.0 1.9 convolution_convert_fusion.2
  355.9 2.0 reshape.156
  357.9 1.4 broadcast_in_dim.86
  359.4 30.7 %all_to_all.66 = bf16[32,2,6144]{2,1,0:T(2,128)(2,1)} all-to-all(bf16[32,2,6144]{2,1,0:T(2,128)(2,1)S(1)} %bitcast.171), channel_id=1, replica_groups=mesh['seg'=8,'ep_0'=8,'ep_1'=4] {'ep_0','ep_1'}, dimensions={0} | all-to-all | bytes 1572864 | tf_op jit(solution)/shard_map/all_to_all | solution.py:162
  390.1 3.0 reshape.158
  393.1 40.3 %all-gather.5.cloned.1.call-done = bf16[512,6144]{1,0:T(8,128)(2,1)} async-done(((bf16[64,6144]{1,0:T(8,128)(2,1)}), bf16[512,6144]{1,0:T(8,128)(2,1)}) %all-gather.5.cloned.1.call-update) | async-done | bytes 6291472 | tf_op jit(solution)/shard_map/all_gather | solution.py:165
  433.4 12.0 %convolution_convert_fusion = bf16[512,6144]{1,0:T(8,128)(2,1)} fusion(bf16[1,288,6144]{2,1,0:T(8,128)(2,1)S(1)} %copy-done, bf16[512,6144]{1,0:T(8,128)(2,1)} %all-gather.5.cloned.1.call-done, bf16[1,6144,288]{1,2,0:T(8,128)(2,1)} %param.20), kind=kOutput, calls=%fused_computation.10 | convolution fusion | flops 3627761664 | bytes 19660800 | tf_op jit(solution)/shard_map/dot_general | solution.py:65
  445.5 2.5 all_to_all.54
  448.0 10.2 %all-to-all-start.3 = ((bf16[32,64,256]{2,1,0:T(8,128)(2,1)}), bf16[32,64,256]{2,1,0:T(8,128)(2,1)}, u32[]{:S(2)}, u32[]{:S(2)}) async-start(bf16[32,64,256]{2,1,0:T(8,128)(2,1)} %all_to_all.54), calls=%async_computation.3 | async-start | bytes 2097152 | tf_op jit(solution)/shard_map/all_to_all | solution.py:130
  458.3 28.5 %all-to-all-done.3 = bf16[32,64,256]{2,1,0:T(8,128)(2,1)} async-done(((bf16[32,64,256]{2,1,0:T(8,128)(2,1)}), bf16[32,64,256]{2,1,0:T(8,128)(2,1)}, u32[]{:S(2)}, u32[]{:S(2)}) %all-to-all-start.3) | async-done | bytes 1048608 | tf_op jit(solution)/shard_map/all_to_all | solution.py:130
  486.8 1.5 convert_bitcast_fusion
  488.3 1.5 copy.163
  489.8 1.6 fusion.15
  491.4 2.9 convert_element_type.93
  494.2 9.8 %all-to-all-start.6 = ((bf16[32,2,6144]{2,1,0:T(2,128)(2,1)}), bf16[32,2,6144]{2,1,0:T(2,128)(2,1)}, u32[]{:S(2)}, u32[]{:S(2)}) async-start(bf16[32,2,6144]{2,1,0:T(2,128)(2,1)} %convert_element_type.93), calls=%async_computation.9 | async-start | bytes 1572864 | tf_op jit(solution)/shard_map/all_to_all | solution.py:172
  504.1 2.8 multiply_convert_fusion.1
  506.9 18.8 %all-to-all-done.6 = bf16[32,2,6144]{2,1,0:T(2,128)(2,1)} async-done(((bf16[32,2,6144]{2,1,0:T(2,128)(2,1)}), bf16[32,2,6144]{2,1,0:T(2,128)(2,1)}, u32[]{:S(2)}, u32[]{:S(2)}) %all-to-all-start.6) | async-done | bytes 786464 | tf_op jit(solution)/shard_map/all_to_all | solution.py:172
  525.7 2.0 convert.7
  528.8 1.9 add.80
  530.7 1.8 fusion.40
  (115 shorter events, 74.8 us)
Async XLA Ops:
  7.2 426.3 %copy-start = (bf16[1,288,6144]{2,1,0:T(8,128)(2,1)S(1)}, bf16[1,288,6144]{2,1,0:T(8,128)(2,1)}, u32[]{:S(2)}) copy-start(bf16[1,288,6144]{2,1,0:T(8,128)(2,1)} %param.21) | copy-start | bytes 10616836
  9.7 66.0 %copy-start.5 = (f32[2048,2]{0,1:T(2,128)S(1)}, f32[2048,2]{0,1:T(2,128)}, u32[]{:S(2)}) copy-start(f32[2048,2]{0,1:T(2,128)} %param.15) | copy-start | bytes 49156
  9.7 55.4 %all-to-all-start.2 = ((bf16[64,32,256]{2,0,1:T(8,128)(2,1)}), bf16[64,32,256]{2,0,1:T(8,128)(2,1)}, u32[]{:S(2)}, u32[]{:S(2)}) async-start(bf16[64,32,256]{2,0,1:T(8,128)(2,1)} %bitcast.169), calls=%async_computation.2 | async-start | bytes 2097152 | tf_op jit(solution)/shard_map/all_to_all | solution.py:77
  65.0 37.4 %all-to-all-start.1 = ((bf16[32,64,256]{2,1,0:T(8,128)(2,1)}), bf16[32,64,256]{2,1,0:T(8,128)(2,1)}, u32[]{:S(2)}, u32[]{:S(2)}) async-start(bf16[32,64,256]{2,1,0:T(8,128)(2,1)} %constant_dynamic-update-slice_fusion), calls=%async_computation.1 | async-start | bytes 2097152 | tf_op jit(solution)/shard_map/all_to_all | solution.py:15
  74.9 209.0 %all-gather.3.cloned.1.call-start = ((), (), s32[]{:S(2)}) async-start(), calls=%async_computation.10 | async-start | bytes 3538944 | tf_op jit(solution)/shard_map/all_gather | solution.py:146
  102.4 39.1 %all-to-all-start = ((bf16[64,32,256]{2,0,1:T(8,128)(2,1)}), bf16[64,32,256]{2,0,1:T(8,128)(2,1)}, u32[]{:S(2)}, u32[]{:S(2)}) async-start(bf16[64,32,256]{2,0,1:T(8,128)(2,1)} %bitcast.170), calls=%async_computation | async-start | bytes 2097152 | tf_op jit(solution)/shard_map/all_to_all | solution.py:75
  110.2 5.7 %copy-start.1 = (bf16[2048,2,128]{2,1,0:T(2,128)(2,1)S(1)}, bf16[2048,2,128]{2,1,0:T(2,128)(2,1)}, u32[]{:S(2)}) copy-start(bf16[2048,2,128]{2,1,0:T(2,128)(2,1)} %reshape.151) | copy-start | bytes 3145732
  118.6 18.7 %copy-start.2 = (bf16[2048,2,128]{2,1,0:T(2,128)(2,1)S(1)}, bf16[2048,2,128]{2,1,0:T(2,128)(2,1)}, u32[]{:S(2)}) copy-start(bf16[2048,2,128]{2,1,0:T(2,128)(2,1)} %reshape.151) | copy-start | bytes 3145732
  138.6 7.4 %copy-start.8 = (bf16[8,2,1]{0,1,2:T(2,128)(2,1)}, bf16[8,2,1]{0,1,2:T(2,128)(2,1)S(1)}, u32[]{:S(2)}) copy-start(bf16[8,2,1]{0,1,2:T(2,128)(2,1)S(1)} %copy.152) | copy-start | bytes 100
  245.5 6.7 %copy-start.4 = (f32[2048,2]{0,1:T(2,128)S(1)}, f32[2048,2]{0,1:T(2,128)}, u32[]{:S(2)}) copy-start(f32[2048,2]{0,1:T(2,128)} %get-tuple-element.131) | copy-start | bytes 49156
  263.1 0.7 copy-start.3
  264.6 18.5 %all-to-all-start.4 = ((f32[32,1,256]{2,1,0:T(1,128)}), f32[32,1,256]{2,1,0:T(1,128)}, u32[]{:S(2)}, u32[]{:S(2)}) async-start(f32[32,1,256]{2,1,0:T(1,128)} %broadcast_in_dim.85), calls=%async_computation.4 | async-start | bytes 65536 | tf_op jit(solution)/shard_map/all_to_all | solution.py:32
  274.4 56.2 %reduce-scatter.4.cloned.1.call-start = ((), (), s32[]{:S(2)}) async-start(), calls=%async_computation.11 | async-start | bytes 3538944 | tf_op jit(solution)/shard_map/reduce_scatter | solution.py:41
  288.6 42.3 %copy-start.6 = (s32[8,2]{0,1:T(2,128)S(1)}, s32[8,2]{0,1:T(2,128)}, u32[]{:S(2)}) copy-start(s32[8,2]{0,1:T(2,128)} %param.18) | copy-start | bytes 196
  288.7 65.3 %reduce-scatter.6.cloned.1.call-start = ((), (), s32[]{:S(2)}) async-start(), calls=%async_computation.12 | async-start | bytes 491520 | tf_op jit(solution)/shard_map/reduce_scatter | solution.py:41
  330.7 102.8 %all-gather.5.cloned.1.call-start = ((), (), s32[]{:S(2)}) async-start(), calls=%async_computation.13 | async-start | bytes 7077888 | tf_op jit(solution)/shard_map/all_gather | solution.py:165
  393.1 98.3 %reduce-scatter.8.cloned.1.call-start = ((), (), s32[]{:S(2)}) async-start(), calls=%async_computation.14 | async-start | bytes 7077888 | tf_op jit(solution)/shard_map/reduce_scatter | solution.py:166
  445.5 12.8 %copy-start.7 = (f32[8,2]{0,1:T(2,128)S(1)}, f32[8,2]{0,1:T(2,128)}, u32[]{:S(2)}) copy-start(f32[8,2]{0,1:T(2,128)} %param.19) | copy-start | bytes 196
  448.0 38.7 %all-to-all-start.3 = ((bf16[32,64,256]{2,1,0:T(8,128)(2,1)}), bf16[32,64,256]{2,1,0:T(8,128)(2,1)}, u32[]{:S(2)}, u32[]{:S(2)}) async-start(bf16[32,64,256]{2,1,0:T(8,128)(2,1)} %all_to_all.54), calls=%async_computation.3 | async-start | bytes 2097152 | tf_op jit(solution)/shard_map/all_to_all | solution.py:130
  494.2 31.5 %all-to-all-start.6 = ((bf16[32,2,6144]{2,1,0:T(2,128)(2,1)}), bf16[32,2,6144]{2,1,0:T(2,128)(2,1)}, u32[]{:S(2)}, u32[]{:S(2)}) async-start(bf16[32,2,6144]{2,1,0:T(2,128)(2,1)} %convert_element_type.93), calls=%async_computation.9 | async-start | bytes 1572864 | tf_op jit(solution)/shard_map/all_to_all | solution.py:172
Sparse Core Ops, SparseCore 0:
  77.6 31.4 all-gather.2
  288.8 41.8 reduce-scatter.3
  333.2 20.7 reduce-scatter.5
  393.2 40.1 all-gather.4
  445.6 45.5 reduce-scatter.7
